TPU v7x, 32 devices: a whole 2x2x4 slice. The times are simulated.
32 devices in a mesh: blk: 4 (over y, x), rep: 8 (over z, core).
Axes of the slice: x: 2, y: 2, z: 4, core: 2. Of those that a mesh axis runs over, the one named last changes fastest.
Arguments:
- image_feats: bfloat16 [8, 2048, 1024], P('rep', 'blk'), may hold values from -6 to 6
- text_feats: bfloat16 [8, 2048, 768], P('rep', 'blk'), may hold values from -6 to 6
- image_head: bfloat16 [1024, 768], replicated, may hold values from -0.1875 to 0.1875
- text_head: bfloat16 [768, 768], replicated, may hold values from -0.21875 to 0.21875
- image_lse: float32 [8, 2048], P('rep', 'blk'), as said below
- text_lse: float32 [8, 2048], P('rep', 'blk'), as said below
Outputs:
- image_feat_grad: float32 [8, 2048, 1024], P('rep', 'blk')
- text_feat_grad: float32 [8, 2048, 768], P('rep', 'blk')
- image_head_grad: float32 [1024, 768], replicated
- text_head_grad: float32 [768, 768], replicated
Inputs may be any that keep to these rules, and one draw needn't show every extreme that they name: `image_lse`: each entry lies between ln(2048) + 1 and ln(2048) + 2.5. `text_lse`: each entry lies between ln(2048) + 1 and ln(2048) + 2.5.
All inputs are finite; a program needn't handle non-finite values.
Results may differ from a plain program's by a relative error of at most 0.028.
Values may be sent and summed in bfloat16 or wider, within the bound.
A program may use at most 128 MiB of HBM per device.

v0:
```python
import jax
import jax.numpy as jnp
from jax import lax
from jax.sharding import PartitionSpec as P

logit_scale = 50.0
epsilon = 1e-06


def project_head(feats, weight):
    raw = jnp.dot(feats, weight, preferred_element_type=jnp.float32)
    factor = lax.rsqrt(jnp.sum(raw * raw, axis=1, keepdims=True) + epsilon)
    return (raw * factor, factor)


def pre_gradient(embed, factor, grad):
    inner = jnp.sum(embed * grad, axis=1, keepdims=True)
    return (factor * (grad - embed * inner)).astype(jnp.bfloat16)


def weight_tile(left, left_lse, right, right_lse):
    scores = logit_scale * lax.dot_general(
        left, right, (((1,), (1,)), ((), ())), preferred_element_type=jnp.float32
    )
    return (
        0.5 * (jnp.exp(scores - left_lse[:, None]) + jnp.exp(scores - right_lse[None, :]))
    ).astype(jnp.bfloat16)


def shards(image_feats, text_feats, image_head, text_head, image_lse, text_lse):
    image_rows = image_feats[0]
    text_rows = text_feats[0]
    lse_img = image_lse[0]
    lse_txt = text_lse[0]
    image_embed, image_scale = project_head(image_rows, image_head)
    text_embed, text_scale = project_head(text_rows, text_head)
    image_round = image_embed.astype(jnp.bfloat16)
    text_round = text_embed.astype(jnp.bfloat16)
    image_piece = lax.all_gather(image_round, "blk", axis=0, tiled=True)
    image_piece_lse = lax.all_gather(
        lse_img.astype(jnp.bfloat16), "blk", axis=0, tiled=True
    ).astype(jnp.float32)
    text_piece = lax.all_gather(text_round, "blk", axis=0, tiled=True)
    text_piece_lse = lax.all_gather(lse_txt.astype(jnp.bfloat16), "blk", axis=0, tiled=True).astype(
        jnp.float32
    )
    image_weights = weight_tile(image_round, lse_img, text_piece, text_piece_lse)
    image_total_part = jnp.dot(image_weights, text_piece, preferred_element_type=jnp.float32)
    text_weights = weight_tile(image_piece, image_piece_lse, text_round, lse_txt)
    text_total_part = lax.dot_general(
        text_weights, image_piece, (((0,), (0,)), ((), ())), preferred_element_type=jnp.float32
    )
    image_grad = logit_scale * image_total_part - logit_scale * text_round.astype(jnp.float32)
    text_grad = logit_scale * text_total_part - logit_scale * image_round.astype(jnp.float32)
    image_pre = pre_gradient(image_embed, image_scale, image_grad)
    text_pre = pre_gradient(text_embed, text_scale, text_grad)
    image_back = lax.dot_general(
        image_pre, image_head, (((1,), (1,)), ((), ())), preferred_element_type=jnp.float32
    )
    text_back = lax.dot_general(
        text_pre, text_head, (((1,), (1,)), ((), ())), preferred_element_type=jnp.float32
    )
    image_wgrad = lax.dot_general(
        image_rows, image_pre, (((0,), (0,)), ((), ())), preferred_element_type=jnp.float32
    )
    text_wgrad = lax.dot_general(
        text_rows, text_pre, (((0,), (0,)), ((), ())), preferred_element_type=jnp.float32
    )
    image_total, text_total = lax.psum((image_wgrad, text_wgrad), ("blk", "rep"))
    return (image_back[None], text_back[None], image_total, text_total)


def solution(mesh):
    return jax.shard_map(
        shards,
        mesh=mesh,
        in_specs=(
            P("rep", "blk", None),
            P("rep", "blk", None),
            P(),
            P(),
            P("rep", "blk"),
            P("rep", "blk"),
        ),
        out_specs=(P("rep", "blk", None), P("rep", "blk", None), P(), P()),
        check_vma=False,
    )
```

profile of v0, /device:TPU:0, one launch (start us, length us, event | category | flops | bytes accessed | tf_op | source)
XLA Modules:
  0.0 281.9 jit_solution(11065053901846281296)
XLA Ops:
  7.2 0.0 copy-start
  7.2 0.0 all-gather.7.cloned.1.call-start
  7.2 1.4 copy-done
  8.6 2.3 multiply_reduce_fusion.3
  10.9 1.1 multiply_convert_fusion.5
  11.9 0.0 all-gather.7.cloned.1.call-update
  12.0 0.0 all-gather.5.cloned.1.call-start
  12.0 2.4 multiply_reduce_fusion.2
  14.4 0.0 copy-start.1
  14.4 1.1 copy-done.1
  15.5 0.0 copy-start.9
  15.5 0.0 copy-start.8
  15.5 1.0 multiply_convert_fusion.4
  16.6 0.0 all-gather.5.cloned.1.call-update
  16.6 0.0 all-reduce.3.cloned.1.call-start
  16.7 0.0 copy-done.9
  16.7 9.6 %all-gather.1 = bf16[4,1,512]{2,1,0:T(2,128)(2,1)S(1)} all-gather(bf16[1,1,512]{2,1,0:T(2,128)(2,1)S(1)} %reshape.27), channel_id=1, replica_groups=mesh['blk'=4,'rep'=8] {'blk'}, dimensions={0}, use_global_device_ids=true | all-gather | bytes 5120 | tf_op jit(solution)/shard_map/all_gather | solution.py:40
  26.3 0.0 copy-done.8
  26.3 8.4 %all-gather = bf16[4,1,512]{2,1,0:T(2,128)(2,1)S(1)} all-gather(bf16[1,1,512]{2,1,0:T(2,128)(2,1)S(1)} %reshape.25), channel_id=1, replica_groups=mesh['blk'=4,'rep'=8] {'blk'}, dimensions={0}, use_global_device_ids=true | all-gather | bytes 5120 | tf_op jit(solution)/shard_map/all_gather | solution.py:44
  34.7 24.1 %all-gather.7.cloned.1.call-done = bf16[2048,768]{1,0:T(8,128)(2,1)} async-done(((bf16[512,768]{1,0:T(8,128)(2,1)}), bf16[2048,768]{1,0:T(8,128)(2,1)}) %all-gather.7.cloned.1.call-update) | async-done | bytes 3145744 | tf_op jit(solution)/shard_map/all_gather | solution.py:39
  58.8 9.4 %multiply_reduce_fusion = (f32[512]{0:T(512)S(1)}, f32[512,768]{1,0:T(8,128)}) fusion(f32[512,768]{1,0:T(8,128)} %copy-done.1, f32[512]{0:T(512)S(1)} %add_rsqrt_fusion, bf16[512,768]{1,0:T(8,128)(2,1)} %multiply_convert_fusion.5, bf16[2048,768]{1,0:T(8,128)(2,1)} %all-gather.7.cloned.1.call-done, bf16[512,768]{1,0:T(8,128)(2,1)} %multiply_convert_fusion.4, ...), kind=kOutput, calls=%fused_computation.6 | convolution fusion | flops 3230268928 | bytes 7878656 | tf_op jit(solution)/shard_map/dot_general | solution.py:50
  68.2 0.0 copy-start.7
  68.2 2.5 multiply_convert_fusion.2
  70.7 0.0 copy-start.2
  70.7 0.9 copy-done.2
  71.5 0.0 copy-done.7
  71.5 2.2 convolution_bitcast_fusion.1
  73.8 31.3 %all-gather.5.cloned.1.call-done = bf16[2048,768]{1,0:T(8,128)(2,1)} async-done(((bf16[512,768]{1,0:T(8,128)(2,1)}), bf16[2048,768]{1,0:T(8,128)(2,1)}) %all-gather.5.cloned.1.call-update) | async-done | bytes 3145744 | tf_op jit(solution)/shard_map/all_gather | solution.py:43
  105.1 8.1 %multiply_reduce_fusion.1 = (f32[512]{0:T(512)S(1)}, f32[512,768]{1,0:T(8,128)}) fusion(f32[512,768]{1,0:T(8,128)S(1)} %get-tuple-element.17, f32[512]{0:T(512)S(1)} %add_rsqrt_fusion.1, bf16[512,768]{1,0:T(8,128)(2,1)} %multiply_convert_fusion.4, bf16[2048,768]{1,0:T(8,128)(2,1)} %all-gather.5.cloned.1.call-done, ...), kind=kOutput, calls=%fused_computation.9 | convolution fusion | flops 3230268928 | bytes 7878656 | tf_op jit(solution)/shard_map/dot_general | solution.py:48
  113.2 0.0 copy-start.6
  113.2 1.8 multiply_convert_fusion.3
  115.0 0.0 copy-start.4
  115.0 0.9 copy-done.4
  115.8 0.0 copy-done.6
  115.8 2.7 convolution_bitcast_fusion
  118.5 0.0 copy-start.3
  118.5 0.0 all-reduce.3.cloned.1.call-update
  118.5 1.1 copy-done.3
  119.7 0.0 copy-start.5
  119.7 3.3 %convolution_bitcast_fusion.3 = f32[1,512,768]{2,1,0:T(8,128)} fusion(bf16[512,768]{1,0:T(8,128)(2,1)S(1)} %copy-done.3, bf16[768,768]{1,0:T(8,128)(2,1)} %param.9), kind=kOutput, calls=%fused_computation.13 | convolution fusion | flops 603979776 | bytes 3538944 | tf_op jit(solution)/shard_map/dot_general | solution.py:60
  123.0 0.0 copy-done.5
  123.0 2.3 convolution_bitcast_fusion.2
  125.3 143.5 %all-reduce.3.cloned.1.call-done = (f32[1024,768]{0,1:T(8,128)}, f32[768,768]{0,1:T(8,128)}) async-done(((f32[1024,768]{0,1:T(8,128)}, f32[768,768]{0,1:T(8,128)}), (f32[1024,768]{0,1:T(8,128)}, f32[768,768]{0,1:T(8,128)})) %all-reduce.3.cloned.1.call-update) | async-done | bytes 5505040 | tf_op jit(solution)/shard_map/psum | solution.py:69
  268.8 3.5 %copy.12 = f32[1024,768]{1,0:T(8,128)} copy(f32[1024,768]{0,1:T(8,128)} %get-tuple-element.12) | data formatting | bytes 6291456
  272.3 3.0 %copy.13 = f32[768,768]{1,0:T(8,128)} copy(f32[768,768]{0,1:T(8,128)} %get-tuple-element.13) | data formatting | bytes 4718592
  (8 shorter events, 0.0 us)
Async XLA Ops:
  7.2 1.4 copy-start
  7.2 51.6 %all-gather.7.cloned.1.call-start = ((), (), s32[]{:S(2)}) async-start(), calls=%async_computation.1 | async-start | bytes 3932160 | tf_op jit(solution)/shard_map/all_gather | solution.py:39
  12.0 93.1 %all-gather.5.cloned.1.call-start = ((), (), s32[]{:S(2)}) async-start(), calls=%async_computation | async-start | bytes 3932160 | tf_op jit(solution)/shard_map/all_gather | solution.py:43
  14.4 1.1 copy-start.1
  15.5 1.1 copy-start.9
  15.5 10.7 %copy-start.8 = (f32[1,512]{1,0:T(1,128)S(1)}, f32[1,512]{1,0:T(1,128)}, u32[]{:S(2)}) copy-start(f32[1,512]{1,0:T(1,128)} %param.11) | copy-start | bytes 6148
  16.6 252.2 %all-reduce.3.cloned.1.call-start = ((), (), s32[]{:S(2)}) async-start(), calls=%async_computation.2 | async-start | bytes 11010048 | tf_op jit(solution)/shard_map/psum | solution.py:69
  68.2 3.4 %copy-start.7 = (bf16[1,512,768]{2,1,0:T(8,128)(2,1)S(1)}, bf16[1,512,768]{2,1,0:T(8,128)(2,1)}, u32[]{:S(2)}) copy-start(bf16[1,512,768]{2,1,0:T(8,128)(2,1)} %param.7) | copy-start | bytes 2359300
  70.7 0.9 copy-start.2
  113.2 2.7 copy-start.6
  115.0 0.9 copy-start.4
  118.5 1.1 copy-start.3
  119.7 3.3 %copy-start.5 = (bf16[512,768]{1,0:T(8,128)(2,1)S(1)}, bf16[512,768]{1,0:T(8,128)(2,1)}, u32[]{:S(2)}) copy-start(bf16[512,768]{1,0:T(8,128)(2,1)} %copy-done.4) | copy-start | bytes 2359300
Sparse Core Ops, SparseCore 0:
  12.1 46.6 all-gather.6
  61.2 43.8 all-gather.4
  118.7 150.0 all-reduce.2
where the time goes:
time: 282 us
  waiting for transfers between devices  199 us (71%)
  matrix products  32.7 us (12%)
  blocking collectives  18 us (6%)
  between operations  13.9 us (5%)
  local copies, waits for them, and re-layouts  12 us (4%)
  other arithmetic  6.39 us (2%)
    psum x1, waiting for transfers between devices, shards(): lax.psum((image_wgrad, text_wgrad), ('blk', 'rep'))  143 us
    all_gather x1, waiting for transfers between devices, shards(): text_piece = lax.all_gather(text_round, 'blk', axis=0, tiled=True)  31.3 us
    all_gather x1, waiting for transfers between devices, shards(): image_piece = lax.all_gather(image_round, 'blk', axis=0, tiled=True)  24.1 us
    unnamed x24, local copies, waits for them, and re-layouts  12 us
    all_gather x1, blocking collectives, shards(): lax.all_gather(lse_img.astype(jnp.bfloat16), 'blk', axis=0, tiled=True)  9.58 us
    dot_general x1, matrix products, shards(): lax.dot_general(text_weights, image_piece, (((0,), (0,)), ((), ())), pref...  9.41 us
    all_gather x1, blocking collectives, shards(): lax.all_gather(lse_txt.astype(jnp.bfloat16), 'blk', axis=0, tiled=True)  8.38 us
    dot_general x1, matrix products, shards(): jnp.dot(image_weights, text_piece, preferred_element_type=jnp.float32)  8.08 us
  transfers between devices with their start and end apart: 3, of which 3 were waited for; matrix products, arithmetic and copies ran while one was open for 8% of the time, Pallas kernels for 0%

commit v1 on v0

--- a/solution.py
+++ b/solution.py
@@ -66,7 +66,7 @@
     text_wgrad = lax.dot_general(
         text_rows, text_pre, (((0,), (0,)), ((), ())), preferred_element_type=jnp.float32
     )
-    image_total, text_total = lax.psum((image_wgrad, text_wgrad), ("blk", "rep"))
+    image_total, text_total = lax.psum(lax.psum((image_wgrad, text_wgrad), "rep"), "blk")
     return (image_back[None], text_back[None], image_total, text_total)
 
 

time: 282 us -> 382 us (1.35)
  waiting for transfers between devices: 199 us -> 299 us
    psum x1 -> x2, waiting for transfers between devices: 143 us -> 243 us  [the longest x1 122 us: shards(): lax.psum(lax.psum((image_wgrad, text_wgrad), 'rep'), 'blk')]
  transfers between devices with their start and end apart: 3 -> 4, of which waited for: 3 -> 4; matrix products, arithmetic and copies ran while one was open for 8% -> 6% of each run, Pallas kernels for 0% -> 0%
where the time goes in v1:
time: 382 us
  waiting for transfers between devices  299 us (78%)
  matrix products  32.7 us (9%)
  blocking collectives  18 us (5%)
  between operations  13.9 us (4%)
  local copies, waits for them, and re-layouts  11.9 us (3%)
  other arithmetic  6.38 us (2%)
    psum x1, waiting for transfers between devices, shards(): lax.psum(lax.psum((image_wgrad, text_wgrad), 'rep'), 'blk')  122 us
    psum x1, waiting for transfers between devices, shards(): lax.psum((image_wgrad, text_wgrad), 'rep')  121 us
    all_gather x1, waiting for transfers between devices, shards(): text_piece = lax.all_gather(text_round, 'blk', axis=0, tiled=True)  31.3 us
    all_gather x1, waiting for transfers between devices, shards(): image_piece = lax.all_gather(image_round, 'blk', axis=0, tiled=True)  24.1 us
    unnamed x24, local copies, waits for them, and re-layouts  11.9 us
    all_gather x1, blocking collectives, shards(): lax.all_gather(lse_img.astype(jnp.bfloat16), 'blk', axis=0, tiled=True)  9.58 us
    dot_general x1, matrix products, shards(): lax.dot_general(text_weights, image_piece, (((0,), (0,)), ((), ())), pref...  9.45 us
    all_gather x1, blocking collectives, shards(): lax.all_gather(lse_txt.astype(jnp.bfloat16), 'blk', axis=0, tiled=True)  8.38 us
  transfers between devices with their start and end apart: 4, of which 4 were waited for; matrix products, arithmetic and copies ran while one was open for 6% of the time, Pallas kernels for 0%

profile of v1, /device:TPU:0, one launch (start us, length us, event | category | flops | bytes accessed | tf_op | source)
XLA Modules:
  0.0 381.7 jit_solution(17092669733265559306)
XLA Ops:
  7.2 0.0 copy-start
  7.2 0.0 all-gather.7.cloned.1.call-start
  7.2 1.4 copy-done
  8.6 2.3 multiply_reduce_fusion.3
  10.9 1.1 multiply_convert_fusion.5
  11.9 0.0 all-gather.7.cloned.1.call-update
  12.0 0.0 all-gather.5.cloned.1.call-start
  12.0 2.4 multiply_reduce_fusion.2
  14.4 0.0 copy-start.1
  14.4 1.1 copy-done.1
  15.5 0.0 copy-start.9
  15.5 0.0 copy-start.8
  15.5 1.0 multiply_convert_fusion.4
  16.6 0.0 all-gather.5.cloned.1.call-update
  16.6 0.0 all-reduce.5.cloned.1.call-start
  16.6 0.0 copy-done.9
  16.7 9.6 %all-gather.1 = bf16[4,1,512]{2,1,0:T(2,128)(2,1)S(1)} all-gather(bf16[1,1,512]{2,1,0:T(2,128)(2,1)S(1)} %reshape.27), channel_id=1, replica_groups=mesh['blk'=4,'rep'=8] {'blk'}, dimensions={0}, use_global_device_ids=true | all-gather | bytes 5120 | tf_op jit(solution)/shard_map/all_gather | solution.py:40
  26.3 0.0 copy-done.8
  26.3 8.4 %all-gather = bf16[4,1,512]{2,1,0:T(2,128)(2,1)S(1)} all-gather(bf16[1,1,512]{2,1,0:T(2,128)(2,1)S(1)} %reshape.25), channel_id=1, replica_groups=mesh['blk'=4,'rep'=8] {'blk'}, dimensions={0}, use_global_device_ids=true | all-gather | bytes 5120 | tf_op jit(solution)/shard_map/all_gather | solution.py:44
  34.7 24.1 %all-gather.7.cloned.1.call-done = bf16[2048,768]{1,0:T(8,128)(2,1)} async-done(((bf16[512,768]{1,0:T(8,128)(2,1)}), bf16[2048,768]{1,0:T(8,128)(2,1)}) %all-gather.7.cloned.1.call-update) | async-done | bytes 3145744 | tf_op jit(solution)/shard_map/all_gather | solution.py:39
  58.8 9.4 %multiply_reduce_fusion = (f32[512]{0:T(512)S(1)}, f32[512,768]{1,0:T(8,128)}) fusion(f32[512,768]{1,0:T(8,128)} %copy-done.1, f32[512]{0:T(512)S(1)} %add_rsqrt_fusion, bf16[512,768]{1,0:T(8,128)(2,1)} %multiply_convert_fusion.5, bf16[2048,768]{1,0:T(8,128)(2,1)} %all-gather.7.cloned.1.call-done, bf16[512,768]{1,0:T(8,128)(2,1)} %multiply_convert_fusion.4, ...), kind=kOutput, calls=%fused_computation.6 | convolution fusion | flops 3230268928 | bytes 7878656 | tf_op jit(solution)/shard_map/dot_general | solution.py:50
  68.2 0.0 copy-start.7
  68.2 2.5 multiply_convert_fusion.2
  70.7 0.0 copy-start.2
  70.7 0.9 copy-done.2
  71.6 0.0 copy-done.7
  71.6 2.2 convolution_bitcast_fusion.1
  73.8 31.3 %all-gather.5.cloned.1.call-done = bf16[2048,768]{1,0:T(8,128)(2,1)} async-done(((bf16[512,768]{1,0:T(8,128)(2,1)}), bf16[2048,768]{1,0:T(8,128)(2,1)}) %all-gather.5.cloned.1.call-update) | async-done | bytes 3145744 | tf_op jit(solution)/shard_map/all_gather | solution.py:43
  105.1 8.1 %multiply_reduce_fusion.1 = (f32[512]{0:T(512)S(1)}, f32[512,768]{1,0:T(8,128)}) fusion(f32[512,768]{1,0:T(8,128)S(1)} %get-tuple-element.19, f32[512]{0:T(512)S(1)} %add_rsqrt_fusion.1, bf16[512,768]{1,0:T(8,128)(2,1)} %multiply_convert_fusion.4, bf16[2048,768]{1,0:T(8,128)(2,1)} %all-gather.5.cloned.1.call-done, ...), kind=kOutput, calls=%fused_computation.9 | convolution fusion | flops 3230268928 | bytes 7878656 | tf_op jit(solution)/shard_map/dot_general | solution.py:48
  113.2 0.0 copy-start.6
  113.2 1.8 multiply_convert_fusion.3
  115.0 0.0 copy-start.4
  115.0 0.9 copy-done.4
  115.8 0.0 copy-done.6
  115.9 2.7 convolution_bitcast_fusion
  118.5 0.0 all-reduce.5.cloned.1.call-update
  118.5 0.0 all-reduce.7.cloned.1.call-start
  118.6 121.3 %all-reduce.5.cloned.1.call-done = (f32[1024,768]{0,1:T(8,128)}, f32[768,768]{0,1:T(8,128)}) async-done(((f32[1024,768]{0,1:T(8,128)}, f32[768,768]{0,1:T(8,128)}), (f32[1024,768]{0,1:T(8,128)}, f32[768,768]{0,1:T(8,128)})) %all-reduce.5.cloned.1.call-update) | async-done | bytes 5505040 | tf_op jit(solution)/shard_map/psum | solution.py:69
  239.9 0.0 copy-start.3
  239.9 0.0 all-reduce.7.cloned.1.call-update
  239.9 1.1 copy-done.3
  241.0 0.0 copy-start.5
  241.0 3.3 convolution_bitcast_fusion.3
  244.3 0.0 copy-done.5
  244.3 2.3 convolution_bitcast_fusion.2
  246.7 121.9 %all-reduce.7.cloned.1.call-done = (f32[1024,768]{0,1:T(8,128)}, f32[768,768]{0,1:T(8,128)}) async-done(((f32[1024,768]{0,1:T(8,128)}, f32[768,768]{0,1:T(8,128)}), (f32[1024,768]{0,1:T(8,128)}, f32[768,768]{0,1:T(8,128)})) %all-reduce.7.cloned.1.call-update) | async-done | bytes 5505040 | tf_op jit(solution)/shard_map/psum | solution.py:69
  368.6 3.5 copy.12
  372.1 3.0 copy.13
  (8 shorter events, 0.0 us)
Async XLA Ops:
  7.2 1.4 copy-start
  7.2 51.6 %all-gather.7.cloned.1.call-start = ((), (), s32[]{:S(2)}) async-start(), calls=%async_computation.1 | async-start | bytes 3932160 | tf_op jit(solution)/shard_map/all_gather | solution.py:39
  12.0 93.1 %all-gather.5.cloned.1.call-start = ((), (), s32[]{:S(2)}) async-start(), calls=%async_computation | async-start | bytes 3932160 | tf_op jit(solution)/shard_map/all_gather | solution.py:43
  14.4 1.1 copy-start.1
  15.5 1.1 copy-start.9
  15.5 10.7 %copy-start.8 = (f32[1,512]{1,0:T(1,128)S(1)}, f32[1,512]{1,0:T(1,128)}, u32[]{:S(2)}) copy-start(f32[1,512]{1,0:T(1,128)} %param.11) | copy-start | bytes 6148
  16.6 223.3 %all-reduce.5.cloned.1.call-start = ((), (), s32[]{:S(2)}) async-start(), calls=%async_computation.2 | async-start | bytes 11010048 | tf_op jit(solution)/shard_map/psum | solution.py:69
  68.2 3.3 copy-start.7
  70.7 0.9 copy-start.2
  113.2 2.7 copy-start.6
  115.0 0.9 copy-start.4
  118.5 250.0 %all-reduce.7.cloned.1.call-start = ((), (), s32[]{:S(2)}) async-start(), calls=%async_computation.3 | async-start | bytes 11010048 | tf_op jit(solution)/shard_map/psum | solution.py:69
  239.9 1.1 copy-start.3
  241.0 3.3 copy-start.5
Sparse Core Ops, SparseCore 0:
  12.1 46.6 all-gather.6
  61.2 43.8 all-gather.4
  118.7 121.1 all-reduce.4
  243.3 125.2 all-reduce.6
